TPU v7x, 32 devices: a whole 2x2x4 slice. The times are simulated.
32 devices in a mesh: groups: 2 (over x), tensor: 16 (over z, y, core).
Axes of the slice: x: 2, y: 2, z: 4, core: 2. Of those that a mesh axis runs over, the one named last changes fastest.
Arguments:
- tokens: bfloat16 [1024, 8192], P('groups', 'tensor'), parts along dimension 0, may hold values from -6 to 6
- norm_gain: float32 [8192], P('tensor'), may hold values from 0.1 to 1.9
- w_in: bfloat16 [8192, 3, 8192], P(None, None, 'tensor'), may hold values from -0.0625 to 0.0625
- w_short: float32 [3, 3, 8192], P(None, None, 'tensor'), may hold values from -3 to 3
- filters: bfloat16 [512, 128], P('tensor'), may hold values from -0.5 to 0.5
- skip: float32 [8192], P('tensor'), may hold values from -4 to 4
- w_out: bfloat16 [8192, 8192], P('tensor'), may hold values from -0.0625 to 0.0625
Outputs:
- mixed: bfloat16 [1024, 8192], P('groups', 'tensor'), parts along dimension 0
There are 2 independent parts, one for each index of `groups`. A program takes and returns all parts, laid end to end along the dimension named above; an argument that names none is the same for every part. Nothing has to cross between parts.
All inputs are finite; a program needn't handle non-finite values.
Results may differ from a plain program's by a relative error of at most 0.0085.
Values may be sent and summed in bfloat16 or wider, within the bound.
A program may use at most 192 MiB of HBM per device.

v0:
```python
import jax
import jax.numpy as jnp
from jax import lax
from jax.sharding import PartitionSpec as P

D = 8192


def shifted(field, lag):
    pads = ((lag, 0),) + ((0, 0),) * (field.ndim - 1)
    return jnp.pad(field, pads)[: field.shape[0]]


def lag_matrix(filters, rows):
    count, taps = filters.shape
    length = taps + rows
    line = jnp.concatenate([filters, jnp.zeros((count, rows), filters.dtype)], axis=1)
    tiled = jnp.tile(line, (1, rows))[:, : rows * (length - 1)]
    return tiled.reshape(count, rows, length - 1)[:, :, :rows]


def on_device(tokens, norm_gain, w_in, w_short, filters, skip, w_out):
    wide = tokens.astype(jnp.float32)
    squares = lax.psum(jnp.sum(wide * wide, axis=1, keepdims=True), "tensor")
    factor = lax.rsqrt(squares / D + 1e-05)
    normed = (wide * factor * norm_gain[None, :]).astype(jnp.bfloat16)
    width = w_in.shape[0]
    local = w_in.shape[2]
    rows = tokens.shape[0]
    w_flat = w_in.reshape(width, 3 * local)
    chosen = w_flat
    proj = jnp.dot(
        lax.all_gather(normed, "tensor", axis=1, tiled=True),
        chosen,
        preferred_element_type=jnp.float32,
    )
    proj = proj.reshape(rows, 3, local)
    short = w_short[0][None] * proj
    for lag in range(1, w_short.shape[0]):
        short = short + w_short[lag][None] * shifted(proj, lag)
    gated = (short[:, 1] * short[:, 2]).astype(jnp.bfloat16)
    count = filters.shape[0]
    lagged = lag_matrix(filters, rows)
    grouped = gated.reshape(rows, count, local // count)
    conv = jnp.einsum("fst,sfg->tfg", lagged, grouped, preferred_element_type=jnp.float32)
    conv = conv.reshape(rows, local)
    hidden = ((conv + skip[None, :] * gated.astype(jnp.float32)) * short[:, 0]).astype(jnp.bfloat16)
    w_cols = lax.all_to_all(w_out, "tensor", split_axis=1, concat_axis=0, tiled=True)
    chosen = w_cols
    summed = jnp.dot(
        lax.all_gather(hidden, "tensor", axis=1, tiled=True),
        chosen,
        preferred_element_type=jnp.float32,
    )
    return (wide + summed).astype(jnp.bfloat16)


def solution(mesh):
    return jax.shard_map(
        on_device,
        mesh=mesh,
        in_specs=(
            P("groups", "tensor"),
            P("tensor"),
            P(None, None, "tensor"),
            P(None, None, "tensor"),
            P("tensor", None),
            P("tensor"),
            P("tensor", None),
        ),
        out_specs=P("groups", "tensor"),
        check_vma=False,
    )
```

profile of v0, /device:TPU:0, one launch (start us, length us, event | category | flops | bytes accessed | tf_op | source)
XLA Modules:
  0.0 382.9 jit_solution(3870038537014596827)
XLA Ops:
  6.5 0.0 all-gather.3.cloned.1.call-start
  6.5 1.2 fusion.10
  7.8 34.9 %psum.7 = f32[512,1]{0,1:T(1,128)S(1)} all-reduce(f32[512,1]{0,1:T(1,128)S(1)} %bitcast.46), channel_id=1, replica_groups=mesh['groups'=2,'tensor'=16] {'tensor'}, use_global_device_ids=true, to_apply=%region_1.0 | all-reduce | flops 512 | bytes 4096 | tf_op jit(solution)/shard_map/psum | solution.py:24
  42.7 2.0 fusion.12
  44.7 0.0 all-gather.3.cloned.1.call-update
  44.7 12.1 %copy.16 = bf16[512,8192]{0,1:T(8,128)(2,1)} copy(bf16[512,8192]{1,0:T(8,128)(2,1)} %param.13) | data formatting | bytes 16777216 | tf_op args[6]
  56.8 4.8 %all-to-all-start = ((bf16[512,16,512]{0,2,1:T(8,128)(2,1)}), bf16[512,16,512]{0,2,1:T(8,128)(2,1)}, u32[]{:S(2)}, u32[]{:S(2)}) async-start(bf16[512,16,512]{0,2,1:T(8,128)(2,1)} %bitcast.41), calls=%async_computation | async-start | bytes 16777216 | tf_op jit(solution)/shard_map/all_to_all | solution.py:48
  61.6 0.0 copy-start.2
  61.6 0.0 all-gather.5.cloned.1.call-start
  61.6 33.4 %copy.13 = bf16[8192,3,512]{0,2,1:T(8,128)(2,1)} copy(bf16[8192,3,512]{2,0,1:T(8,128)(2,1)} %param.9) | data formatting | bytes 50331648 | tf_op args[2]
  95.1 0.0 copy-done.2
  95.1 2.9 tile.4
  98.0 67.1 %copy.18 = bf16[4,8,512,640]{3,1,2,0:T(8,128)(2,1)S(1)} copy(bf16[4,8,512,640]{3,2,1,0:T(8,128)(2,1)S(1)} %bitcast.39) | data formatting | bytes 41943040
  165.1 8.1 %slice.42 = bf16[32,327168]{1,0:T(8,128)(2,1)} slice(bf16[32,327680]{1,0:T(8,128)(2,1)S(1)} %bitcast.40), slice={[0:32], [0:327168]} | slice | bytes 41877504 | tf_op jit(solution)/shard_map/slice | solution.py:18
  173.2 0.0 copy-start.1
  173.2 69.0 %reshape.30 = bf16[32,512,639]{2,1,0:T(8,128)(2,1)} reshape(bf16[32,327168]{1,0:T(8,128)(2,1)} %slice.42) | data formatting | bytes 41877504 | tf_op jit(solution)/shard_map/reshape | solution.py:19
  242.2 0.0 copy-done.1
  242.2 0.0 all-gather.3.cloned.1.call-done
  242.2 19.6 %fusion = f32[512,3,512]{2,0,1:T(8,128)S(1)} fusion(bf16[8192,3,512]{0,2,1:T(8,128)(2,1)} %copy.13, bf16[512,8192]{1,0:T(8,128)(2,1)} %all-gather.3.cloned.1.call-done), kind=kOutput, calls=%fused_computation | convolution fusion | flops 12884901888 | bytes 36700160 | tf_op jit(solution)/shard_map/dot_general | solution.py:32
  261.8 0.9 fusion.7
  262.8 0.9 fusion.15
  263.7 2.1 copy.14
  265.8 0.0 copy-start.3
  265.8 9.2 %fusion.2 = f32[32,16,512]{2,1,0:T(8,128)} fusion(bf16[512,32,16]{0,2,1:T(8,128)(2,1)} %bitcast.44, bf16[32,512,639]{2,1,0:T(8,128)(2,1)} %reshape.30), kind=kOutput, calls=%fused_computation.2 | convolution fusion | flops 268435456 | bytes 18350080 | tf_op jit(solution)/shard_map/fst,sfg->tfg/dot_general | solution.py:45
  275.0 2.6 copy.15
  277.6 0.0 copy-done.3
  277.6 2.5 fusion.14
  280.1 0.0 all-gather.5.cloned.1.call-update
  280.1 0.0 all-to-all-done
  280.1 0.0 copy-start
  280.2 12.4 %copy.17 = bf16[16,512,512]{2,1,0:T(8,128)(2,1)} copy(bf16[16,512,512]{1,2,0:T(8,128)(2,1)} %bitcast.15) | data formatting | bytes 16777216 | tf_op jit(solution)/shard_map/all_to_all | solution.py:48
  292.6 72.4 %all-gather.5.cloned.1.call-done = bf16[512,8192]{1,0:T(8,128)(2,1)} async-done(((bf16[512,512]{1,0:T(8,128)(2,1)}), bf16[512,8192]{1,0:T(8,128)(2,1)}) %all-gather.5.cloned.1.call-update) | async-done | bytes 8388624 | tf_op jit(solution)/shard_map/all_gather | solution.py:51
  365.0 0.0 copy-done
  365.0 11.0 %fusion.9 = bf16[512,512]{1,0:T(8,128)(2,1)} fusion(bf16[512,8192]{1,0:T(8,128)(2,1)} %all-gather.5.cloned.1.call-done, bf16[8192,512]{1,0:T(8,128)(2,1)} %bitcast.43, bf16[512,512]{1,0:T(8,128)(2,1)S(1)} %copy-done), kind=kOutput, calls=%fused_computation.14 | convolution fusion | flops 4295753728 | bytes 17825792 | tf_op jit(solution)/shard_map/dot_general | solution.py:50
  (3 shorter events, 0.0 us)
Async XLA Ops:
  6.5 235.7 %all-gather.3.cloned.1.call-start = ((), (), s32[]{:S(2)}) async-start(), calls=%async_computation.1 | async-start | bytes 8912896 | tf_op jit(solution)/shard_map/all_gather | solution.py:33
  56.8 223.3 %all-to-all-start = ((bf16[512,16,512]{0,2,1:T(8,128)(2,1)}), bf16[512,16,512]{0,2,1:T(8,128)(2,1)}, u32[]{:S(2)}, u32[]{:S(2)}) async-start(bf16[512,16,512]{0,2,1:T(8,128)(2,1)} %bitcast.41), calls=%async_computation | async-start | bytes 16777216 | tf_op jit(solution)/shard_map/all_to_all | solution.py:48
  61.6 33.5 %copy-start.2 = (bf16[32,128]{1,0:T(8,128)(2,1)S(1)}, bf16[32,128]{1,0:T(8,128)(2,1)}, u32[]{:S(2)}) copy-start(bf16[32,128]{1,0:T(8,128)(2,1)} %param.11) | copy-start | bytes 24580
  61.6 303.4 %all-gather.5.cloned.1.call-start = ((), (), s32[]{:S(2)}) async-start(), calls=%async_computation.2 | async-start | bytes 8912896 | tf_op jit(solution)/shard_map/all_gather | solution.py:51
  173.2 69.0 %copy-start.1 = (f32[3,3,512]{2,1,0:T(4,128)S(1)}, f32[3,3,512]{2,1,0:T(4,128)}, u32[]{:S(2)}) copy-start(f32[3,3,512]{2,1,0:T(4,128)} %param.10) | copy-start | bytes 55300
  265.8 11.8 %copy-start.3 = (f32[512]{0:T(512)S(1)}, f32[512]{0:T(512)}, u32[]{:S(2)}) copy-start(f32[512]{0:T(512)} %param.12) | copy-start | bytes 6148
  280.1 84.9 %copy-start = (bf16[512,512]{1,0:T(8,128)(2,1)S(1)}, bf16[512,512]{1,0:T(8,128)(2,1)}, u32[]{:S(2)}) copy-start(bf16[512,512]{1,0:T(8,128)(2,1)} %param.7) | copy-start | bytes 1572868
Sparse Core Ops, SparseCore 0:
  44.9 190.1 all-gather.2
  280.3 84.7 all-gather.4
where the time goes:
time: 385 us; the launch traced here: 383 us
  local copies, waits for them, and re-layouts  210 us (55%)
  waiting for transfers between devices  72.5 us (19%)
  matrix products  39.9 us (10%)
  blocking collectives  34.9 us (9%)
  between operations  13.5 us (4%)
  other arithmetic  7.65 us (2%)
  starting transfers between devices  4.8 us (1%)
    unnamed x11, local copies, waits for them, and re-layouts  113 us
    all_gather x1, waiting for transfers between devices, on_device(): lax.all_gather(hidden, 'tensor', axis=1, tiled=True)  72.4 us
    reshape x1, local copies, waits for them, and re-layouts, lag_matrix(): return tiled.reshape(count, rows, length - 1)[:, :, :rows]  69 us
    psum x1, blocking collectives, on_device(): squares = lax.psum(jnp.sum(wide * wide, axis=1, keepdims=True), 'tensor')  34.9 us
    dot_general x1, matrix products, on_device(): jnp.dot(lax.all_gather(normed, 'tensor', axis=1, tiled=True), chosen, pre...  19.6 us
    all_to_all x1, local copies, waits for them, and re-layouts, on_device(): lax.all_to_all(w_out, 'tensor', split_axis=1, concat_axis=0, tiled=True)  12.4 us
    dot_general x1, matrix products, on_device(): jnp.dot(lax.all_gather(hidden, 'tensor', axis=1, tiled=True), chosen, pre...  11 us
    dot_general x1, matrix products, on_device(): jnp.einsum('fst,sfg->tfg', lagged, grouped, preferred_element_type=jnp.fl...  9.22 us
  transfers between devices with their start and end apart: 3, of which 1 were waited for; matrix products, arithmetic and copies ran while one was open for 63% of the time, Pallas kernels for 0%

commit v1 on v0

v1 whole, which is shorter than its diff:
```python
import functools

import jax
import jax.numpy as jnp
from jax import lax
from jax.experimental import pallas as pl
from jax.experimental.pallas import tpu as pltpu
from jax.sharding import PartitionSpec as P

MESH = pl.DeviceIdType.MESH
LANES = 128
PIECES = 2


def chip_at(pos, m):
    upper = pos // (m // 2)
    return (1 - upper) * 2 * pos + upper * (2 * (m - 1 - pos) + 1)


def position_of(chip, m):
    odd = chip % 2
    return (1 - odd) * (chip // 2) + odd * (m - 1 - chip // 2)


class Ring:
    def __init__(self, m):
        me = lax.axis_index("tensor")
        self.m = m
        self.core = me % 2
        self.chip = me // 2
        self.pos = position_of(self.chip, m)
        self.next = (
            {"tensor": chip_at((self.pos + 1) % m, m) * 2 + self.core},
            {"tensor": chip_at((self.pos + m - 1) % m, m) * 2 + self.core},
        )
        self.sibling = {"tensor": self.chip * 2 + 1 - self.core}

    def behind(self, side, steps):
        if side == 0:
            return (self.pos + self.m - steps) % self.m
        return (self.pos + steps) % self.m

    def greet(self):
        barrier = pltpu.get_barrier_semaphore()
        for device in self.next + (self.sibling,):
            pl.semaphore_signal(barrier, inc=1, device_id=device, device_id_type=MESH)

    def met(self):
        pl.semaphore_wait(pltpu.get_barrier_semaphore(), 3)


def remote(src, dst, send, recv, device):
    return pltpu.make_async_remote_copy(
        src_ref=src, dst_ref=dst, send_sem=send, recv_sem=recv,
        device_id=device, device_id_type=MESH,
    )


def gather_kernel(
    m, tokens, gain, w_in, w_out, acc, pair,
    xg, wv, w_sem, ring_send, ring_recv, sib_send, sib_recv, own_send, own_recv,
    keep_sem, give_send, give_recv,
):
    rows, width = tokens.shape
    half = rows // 2
    piece = half // PIECES
    ring = Ring(m)
    core = ring.core
    ring.greet()

    def w_copy(d):
        base = pl.multiple_of(chip_at((ring.pos + d) % m, m) * 2 * width, 2 * width)
        part = pl.ds(base, 2 * width)
        return pltpu.make_async_copy(w_in.at[:, part, :], wv.at[:, part, :], w_sem.at[d])

    w_copy(0).start()
    xg[ring.pos, core] = (tokens[...].astype(jnp.float32) * gain[...]).astype(jnp.bfloat16)
    ring.met()

    def span(side, k):
        return pl.ds(side * half + k * piece, piece)

    def hop(s, side, k, q):
        block = xg.at[q, core, span(side, k), :]
        return remote(block, block, ring_send.at[s, side, k], ring_recv.at[s, side, k], ring.next[side])

    def across(s, side, k, q):
        block = xg.at[q, core, span(side, k), :]
        return remote(block, block, sib_send.at[s, side, k], sib_recv.at[s, side, k], ring.sibling)

    def across_in(s, side, k, q):
        block = xg.at[q, 1 - core, span(side, k), :]
        return remote(block, block, sib_send.at[s, side, k], sib_recv.at[s, side, k], ring.sibling)

    for k in range(PIECES):
        for side in range(2):
            hop(0, side, k, ring.pos).start()
    own = remote(xg.at[ring.pos, core], xg.at[ring.pos, core], own_send, own_recv, ring.sibling)
    own.start()
    own_in = remote(xg.at[ring.pos, 1 - core], xg.at[ring.pos, 1 - core], own_send, own_recv, ring.sibling)
    for d in range(1, m // 2 + 1):
        w_copy(d).start()
        if d < m - d:
            w_copy(m - d).start()

    def keep(q):
        base = pl.multiple_of((chip_at(q, m) * 2 + core) * width, width)
        slot = pl.ds(pl.multiple_of(core * width, width), width)
        return pltpu.make_async_copy(w_out.at[:, pl.ds(base, width)], pair.at[q, slot, :], keep_sem.at[q])

    def give(q):
        base = pl.multiple_of((chip_at(q, m) * 2 + 1 - core) * width, width)
        slot = pl.ds(pl.multiple_of(core * width, width), width)
        return remote(w_out.at[:, pl.ds(base, width)], pair.at[q, slot, :], give_send.at[q], give_recv.at[q], ring.sibling)

    def multiply(s, first):
        for side in range(2):
            q = ring.behind(side, s)
            span_rows = pl.ds(side * half, half)
            base = pl.multiple_of(chip_at(q, m) * 2 * width, 2 * width)
            for b in range(3):
                term = jnp.dot(
                    xg[q, 0, span_rows, :], wv[b, pl.ds(base, width), :],
                    preferred_element_type=jnp.float32,
                ) + jnp.dot(
                    xg[q, 1, span_rows, :], wv[b, pl.ds(base + width, width), :],
                    preferred_element_type=jnp.float32,
                )
                if first:
                    acc[b, span_rows, :] = term
                else:
                    acc[b, span_rows, :] += term

    def pass_on(s, last):
        for k in range(PIECES):
            for side in range(2):
                q = ring.behind(side, s + 1)
                hop(s, side, k, q).wait_recv()
                if not last:
                    hop(s + 1, side, k, q).start()
                across(s, side, k, q).start()

    def use(s):
        @pl.when(s <= m // 2)
        def _():
            w_copy(s).wait()

        @pl.when(s < m // 2)
        def _():
            w_copy(m - s).wait()

        for k in range(PIECES):
            for side in range(2):
                across_in(s - 1, side, k, ring.behind(side, s)).wait_recv()
        multiply(s, False)

    w_copy(0).wait()
    own_in.wait_recv()
    multiply(0, True)
    pass_on(0, m == 2)

    def body(s, carry):
        keep(s - 1).start()
        give(s - 1).start()
        use(s)
        pass_on(s, False)
        return carry

    lax.fori_loop(1, m - 2, body, 0)
    for q in range(m - 3, m):
        keep(q).start()
        give(q).start()
    use(m - 2)
    pass_on(m - 2, True)
    use(m - 1)

    own.wait_send()

    def settle(s, carry):
        for k in range(PIECES):
            for side in range(2):
                hop(s, side, k, ring.behind(side, s)).wait_send()
                across(s, side, k, ring.behind(side, s + 1)).wait_send()
        return carry

    lax.fori_loop(0, m - 1, settle, 0)

    def settle_pairs(q, carry):
        keep(q).wait()
        give(q).wait_send()
        slot = pl.ds(pl.multiple_of((1 - core) * width, width), width)
        view = pair.at[q, slot, :]
        remote(view, view, give_send.at[q], give_recv.at[q], ring.sibling).wait_recv()
        return carry

    lax.fori_loop(0, m, settle_pairs, 0)


def scatter_kernel(
    m, taps, group, proj, factor, w_short, line, skip, pair, tokens, out,
    wv, hid, gs, toep, stage, got, w_sem, ring_send, ring_recv, sib_send, sib_recv,
):
    rows, width = tokens.shape
    half = rows // 2
    piece = half // PIECES
    window = 2 * taps
    per_tile = LANES // group
    ring = Ring(m)
    core = ring.core
    ring.greet()
    fetch = pltpu.make_async_copy(pair, wv, w_sem)
    fetch.start()
    gs[0:taps, :] = jnp.zeros((taps, LANES), jnp.bfloat16)
    ring.met()

    def across(j, which):
        view = hid.at[which, :, pl.ds(pl.multiple_of(j * LANES, LANES), LANES)]
        return remote(view, view, sib_send.at[j], sib_recv.at[j], ring.sibling)

    def tile(j, carry):
        lanes = pl.ds(pl.multiple_of(j * LANES, LANES), LANES)
        at_row = lax.broadcasted_iota(jnp.int32, (rows, LANES), 0)

        def short(b):
            x = proj[b, :, lanes] * factor[...]
            total = w_short[0, pl.ds(b, 1), lanes] * x
            for lag in range(1, w_short.shape[0]):
                moved = jnp.where(at_row >= lag, pltpu.roll(x, lag, 0), 0.0)
                total = total + w_short[lag, pl.ds(b, 1), lanes] * moved
            return total

        gs[taps:, :] = (short(1) * short(2)).astype(jnp.bfloat16)
        query = short(0)
        lines = line[pl.ds(pl.multiple_of(j * per_tile, per_tile), per_tile), :]
        for f in range(per_tile):
            spread = jnp.broadcast_to(lines[f : f + 1, :], (taps, window))
            toep[f * taps : (f + 1) * taps, :] = pltpu.roll(
                spread, 0, 1, stride=1, stride_axis=0
            ).astype(jnp.bfloat16)
        owner = lax.broadcasted_iota(jnp.int32, (taps, LANES), 1) // group
        for i in range(rows // taps):
            every = jnp.dot(
                toep[...], gs[i * taps : i * taps + window, :], preferred_element_type=jnp.float32
            )
            conv = every[0:taps]
            for f in range(1, per_tile):
                conv = jnp.where(owner == f, every[f * taps : (f + 1) * taps], conv)
            gated = gs[(i + 1) * taps : (i + 2) * taps, :].astype(jnp.float32)
            part = (conv + skip[:, lanes] * gated) * query[i * taps : (i + 1) * taps]
            hid[core, i * taps : (i + 1) * taps, lanes] = part.astype(jnp.bfloat16)
        across(j, core).start()
        return carry

    tiles = width // LANES
    lax.fori_loop(0, tiles, tile, 0)
    fetch.wait()
    for j in range(tiles):
        across(j, 1 - core).wait_recv()

    def span(k):
        return pl.ds(k * piece, piece)

    def hop(s, side, k):
        return remote(
            stage.at[side, s, span(k), :], got.at[side, s, span(k), :],
            ring_send.at[s, side, k], ring_recv.at[s, side, k], ring.next[side],
        )

    def partial(side, k, q):
        here = pl.ds(side * half + k * piece, piece)
        return jnp.dot(
            hid[0, here, :], wv[q, 0:width, :], preferred_element_type=jnp.float32
        ) + jnp.dot(
            hid[1, here, :], wv[q, width : 2 * width, :], preferred_element_type=jnp.float32
        )

    for k in range(PIECES):
        for side in range(2):
            stage[side, 0, span(k), :] = partial(side, k, ring.behind(side, 1)).astype(jnp.bfloat16)
            hop(0, side, k).start()

    def body(s, carry):
        for k in range(PIECES):
            for side in range(2):
                part = partial(side, k, ring.behind(side, s + 1))
                hop(s - 1, side, k).wait_recv()
                part = part + got[side, s - 1, span(k), :].astype(jnp.float32)
                stage[side, s, span(k), :] = part.astype(jnp.bfloat16)
                hop(s, side, k).start()
        return carry

    lax.fori_loop(1, m - 1, body, 0)
    for k in range(PIECES):
        for side in range(2):
            here = pl.ds(side * half + k * piece, piece)
            part = tokens[here, :].astype(jnp.float32) + partial(side, k, ring.pos)
            hop(m - 2, side, k).wait_recv()
            part = part + got[side, m - 2, span(k), :].astype(jnp.float32)
            out[here, :] = part.astype(jnp.bfloat16)

    def settle(s, carry):
        for k in range(PIECES):
            for side in range(2):
                hop(s, side, k).wait_send()
        return carry

    lax.fori_loop(0, m - 1, settle, 0)
    for j in range(tiles):
        across(j, core).wait_send()


def on_device(n, tokens, norm_gain, w_in, w_short, filters, skip, w_out):
    m = n // 2
    rows, width = tokens.shape
    depth = w_in.shape[0]
    count, taps = filters.shape
    group = width // count
    wide = tokens.astype(jnp.float32)
    squares = lax.psum(jnp.sum(wide * wide, axis=1, keepdims=True), "tensor")
    dma = pltpu.SemaphoreType.DMA
    vmem = pl.BlockSpec(memory_space=pltpu.VMEM)
    hbm = pl.BlockSpec(memory_space=pl.ANY)
    proj, pair = pl.pallas_call(
        functools.partial(gather_kernel, m),
        out_shape=(
            jax.ShapeDtypeStruct((3, rows, width), jnp.float32),
            jax.ShapeDtypeStruct((m, 2 * width, width), jnp.bfloat16),
        ),
        in_specs=[vmem, vmem, hbm, hbm],
        out_specs=(vmem, hbm),
        scratch_shapes=[
            pltpu.VMEM((m, 2, rows, width), jnp.bfloat16),
            pltpu.VMEM((3, depth, width), jnp.bfloat16),
            dma((m,)),
            dma((m - 1, 2, PIECES)),
            dma((m - 1, 2, PIECES)),
            dma((m - 1, 2, PIECES)),
            dma((m - 1, 2, PIECES)),
            dma,
            dma,
            dma((m,)),
            dma((m,)),
            dma((m,)),
        ],
        compiler_params=pltpu.CompilerParams(
            collective_id=0, has_side_effects=True, vmem_limit_bytes=50 << 20
        ),
        cost_estimate=pl.CostEstimate(
            flops=2 * rows * depth * 3 * width,
            bytes_accessed=2 * depth * width * 5,
            transcendentals=0,
        ),
        name="gather_project",
    )(tokens, norm_gain[None, :], jnp.transpose(w_in, (1, 0, 2)), w_out)
    factor = lax.rsqrt(squares / depth + 1e-05)
    flipped = filters[:, ::-1].astype(jnp.float32)
    line = jnp.pad(flipped, ((0, 0), (1, taps - 1)))
    return pl.pallas_call(
        functools.partial(scatter_kernel, m, taps, group),
        out_shape=jax.ShapeDtypeStruct((rows, width), jnp.bfloat16),
        in_specs=[vmem, vmem, vmem, vmem, vmem, hbm, vmem],
        out_specs=vmem,
        scratch_shapes=[
            pltpu.VMEM((m, 2 * width, width), jnp.bfloat16),
            pltpu.VMEM((2, rows, width), jnp.bfloat16),
            pltpu.VMEM((rows + taps, LANES), jnp.bfloat16),
            pltpu.VMEM((LANES // group * taps, 2 * taps), jnp.bfloat16),
            pltpu.VMEM((2, m - 1, rows // 2, width), jnp.bfloat16),
            pltpu.VMEM((2, m - 1, rows // 2, width), jnp.bfloat16),
            dma,
            dma((m - 1, 2, PIECES)),
            dma((m - 1, 2, PIECES)),
            dma((width // LANES,)),
            dma((width // LANES,)),
        ],
        compiler_params=pltpu.CompilerParams(
            collective_id=1, has_side_effects=True, vmem_limit_bytes=40 << 20
        ),
        cost_estimate=pl.CostEstimate(
            flops=2 * rows * depth * width, bytes_accessed=2 * depth * width, transcendentals=0
        ),
        name="filter_scatter",
    )(proj, factor, w_short, line, skip[None, :], pair, tokens)


def solution(mesh):
    return jax.shard_map(
        functools.partial(on_device, mesh.shape["tensor"]),
        mesh=mesh,
        in_specs=(
            P("groups", "tensor"),
            P("tensor"),
            P(None, None, "tensor"),
            P(None, None, "tensor"),
            P("tensor", None),
            P("tensor"),
            P("tensor", None),
        ),
        out_specs=P("groups", "tensor"),
        check_vma=False,
    )
```

time: 385 us -> 260 us (0.68)
  local copies, waits for them, and re-layouts: 210 us -> 6.83 us
  Pallas kernels: 0 us -> 186 us
  waiting for transfers between devices: 72.5 us -> 0 us
  matrix products: 39.9 us -> 0 us
  blocking collectives: 34.9 us -> 65.3 us
  between operations: 13.5 us -> 0.09 us
  other arithmetic: 7.65 us -> 1.34 us
  starting transfers between devices: 4.8 us -> 0 us
    pallas_call x0 -> x2, Pallas kernels: none -> 186 us  [the longest x1 136 us: on_device(): pl.pallas_call(functools.partial(gather_kernel, m), out_shape=(jax.ShapeD...]
    unnamed x11 -> x13, local copies, waits for them, and re-layouts: 113 us -> 5.9 us
    all_gather x2 -> x0, waiting for transfers between devices: 72.5 us -> none  [the longest x1 72.4 us: on_device(): lax.all_gather(hidden, 'tensor', axis=1, tiled=True)]
    reshape x2 -> x0, local copies, waits for them, and re-layouts: 71.6 us -> none  [the longest x1 69 us: lag_matrix(): return tiled.reshape(count, rows, length - 1)[:, :, :rows]]
    dot_general x3 -> x0, matrix products: 39.9 us -> none  [the longest x1 19.6 us: on_device(): jnp.dot(lax.all_gather(normed, 'tensor', axis=1, tiled=True), chosen, pre...]
    psum x1, blocking collectives: 34.9 us -> 65.3 us  [on_device(): squares = lax.psum(jnp.sum(wide * wide, axis=1, keepdims=True), 'tensor')]
    all_to_all x1 -> x0, local copies, waits for them, and re-layouts: 12.4 us -> none  [on_device(): lax.all_to_all(w_out, 'tensor', split_axis=1, concat_axis=0, tiled=True)]
    slice x1 -> x0, local copies, waits for them, and re-layouts: 8.08 us -> none  [lag_matrix(): tiled = jnp.tile(line, (1, rows))[:, :rows * (length - 1)]]
  transfers between devices with their start and end apart: 3 -> 0, of which waited for: 1 -> 0; matrix products, arithmetic and copies ran while one was open for 63% -> 0% of each run, Pallas kernels for 0% -> 0%
where the time goes in v1:
time: 260 us
  Pallas kernels  186 us (72%)
  blocking collectives  65.3 us (25%)
  local copies, waits for them, and re-layouts  6.83 us (3%)
    pallas_call x1, Pallas kernels, on_device(): pl.pallas_call(functools.partial(gather_kernel, m), out_shape=(jax.ShapeD...  136 us
    psum x1, blocking collectives, on_device(): squares = lax.psum(jnp.sum(wide * wide, axis=1, keepdims=True), 'tensor')  65.3 us
    pallas_call x1, Pallas kernels, on_device(): pl.pallas_call(functools.partial(scatter_kernel, m, taps, group), out_sha...  50.1 us
    unnamed x13, local copies, waits for them, and re-layouts  5.9 us

profile of v1, /device:TPU:0, one launch (start us, length us, event | category | flops | bytes accessed | tf_op | source)
XLA Modules:
  0.0 259.5 jit_solution(3821679435594283408)
XLA Ops:
  0.0 1.2 multiply_reduce_fusion
  1.2 0.8 rev.3
  2.0 0.1 pad_convert_fusion.line
  2.1 0.1 copy.9
  2.2 65.3 %psum.7 = f32[512,1]{1,0:T(8,128)S(1)} all-reduce(f32[512,1]{1,0:T(8,128)S(1)} %copy.9), channel_id=1, replica_groups=mesh['groups'=2,'tensor'=16] {'tensor'}, use_global_device_ids=true, to_apply=%region_1.0 | all-reduce | flops 512 | bytes 4096 | tf_op jit(solution)/shard_map/psum | solution.py:319
  67.6 0.0 copy-start
  67.6 1.0 copy-done
  68.7 0.0 copy-start.3
  68.7 0.7 copy-done.3
  69.4 0.0 copy-start.1
  69.4 0.0 copy-start.2
  69.4 0.0 copy-start.4
  69.4 135.8 %gather_project.1 = (f32[3,512,512]{2,1,0:T(8,128)S(1)}, bf16[8,1024,512]{2,1,0:T(8,128)(2,1)}) custom-call(bf16[512,512]{1,0:T(8,128)(2,1)S(1)} %copy-done, f32[1,512]{1,0:T(1,128)S(1)} %bitcast.4, bf16[3,8192,512]{2,1,0:T(8,128)(2,1)} %bitcast.7, bf16[512,8192]{1,0:T(8,128)(2,1)} %w_out.1), custom_call_target="tpu_custom_call" | custom-call | flops 12884901888 | bytes 41943040 | tf_op jit(solution)/shard_map/gather_project/pallas_call | solution.py:323
  205.2 0.0 copy-done.1
  205.2 0.0 copy-done.2
  205.2 0.0 copy-done.4
  205.2 0.0 copy-start.5
  205.3 3.4 %copy-done.5 = bf16[8,1024,512]{2,1,0:T(8,128)(2,1)S(1)} copy-done((bf16[8,1024,512]{2,1,0:T(8,128)(2,1)S(1)}, bf16[8,1024,512]{2,1,0:T(8,128)(2,1)}, u32[]{:S(2)}) %copy-start.5) | copy-done | bytes 8388632
  208.6 50.1 %filter_scatter.1 = bf16[512,512]{1,0:T(8,128)(2,1)S(1)} custom-call(f32[3,512,512]{2,1,0:T(8,128)S(1)} %get-tuple-element.7.proj, f32[512,1]{1,0:T(8,128)S(1)} %add_rsqrt_fusion.factor, f32[3,3,512]{2,1,0:T(4,128)S(1)} %copy-done.2, f32[32,256]{1,0:T(8,128)S(1)} %pad_convert_fusion.line, f32[1,512]{1,0:T(1,128)S(1)} %bitcast.5, ...), custom_call_target="tpu_custom_call" | custom-call | flops 4294967296 | bytes 8388608 | tf_op jit(solution)/shard_map/filter_scatter/pallas_call | solution.py:358
  258.7 0.8 copy.12
  (1 shorter events, 0.0 us)
Async XLA Ops:
  67.6 1.0 copy-start
  68.7 0.7 copy-start.3
  69.4 135.9 %copy-start.1 = (bf16[512,512]{1,0:T(8,128)(2,1)S(1)}, bf16[512,512]{1,0:T(8,128)(2,1)}, u32[]{:S(2)}) copy-start(bf16[512,512]{1,0:T(8,128)(2,1)} %tokens.3) | copy-start | bytes 1572868
  69.4 135.9 %copy-start.2 = (f32[3,3,512]{2,1,0:T(4,128)S(1)}, f32[3,3,512]{2,1,0:T(4,128)}, u32[]{:S(2)}) copy-start(f32[3,3,512]{2,1,0:T(4,128)} %w_short.1) | copy-start | bytes 55300
  69.4 135.9 %copy-start.4 = (f32[512]{0:T(512)S(1)}, f32[512]{0:T(512)}, u32[]{:S(2)}) copy-start(f32[512]{0:T(512)} %param.12) | copy-start | bytes 6148
  205.2 3.4 %copy-start.5 = (bf16[8,1024,512]{2,1,0:T(8,128)(2,1)S(1)}, bf16[8,1024,512]{2,1,0:T(8,128)(2,1)}, u32[]{:S(2)}) copy-start(bf16[8,1024,512]{2,1,0:T(8,128)(2,1)} %get-tuple-element.8.pair) | copy-start | bytes 25165828

commit v2 on v1

v2 whole, which is shorter than its diff:
```python
import functools

import jax
import jax.numpy as jnp
from jax import lax
from jax.experimental import pallas as pl
from jax.experimental.pallas import tpu as pltpu
from jax.sharding import PartitionSpec as P

MESH = pl.DeviceIdType.MESH
LANES = 128
PIECES = 2
HIGHEST = lax.Precision.HIGHEST


def chip_at(pos, m):
    upper = pos // (m // 2)
    return (1 - upper) * 2 * pos + upper * (2 * (m - 1 - pos) + 1)


def position_of(chip, m):
    odd = chip % 2
    return (1 - odd) * (chip // 2) + odd * (m - 1 - chip // 2)


class Ring:
    def __init__(self, m):
        me = lax.axis_index("tensor")
        self.m = m
        self.core = me % 2
        self.chip = me // 2
        self.pos = position_of(self.chip, m)
        self.next = (
            {"tensor": chip_at((self.pos + 1) % m, m) * 2 + self.core},
            {"tensor": chip_at((self.pos + m - 1) % m, m) * 2 + self.core},
        )
        self.sibling = {"tensor": self.chip * 2 + 1 - self.core}

    def behind(self, side, steps):
        if side == 0:
            return (self.pos + self.m - steps) % self.m
        return (self.pos + steps) % self.m

    def greet(self):
        barrier = pltpu.get_barrier_semaphore()
        for device in self.next + (self.sibling,):
            pl.semaphore_signal(barrier, inc=1, device_id=device, device_id_type=MESH)

    def met(self):
        pl.semaphore_wait(pltpu.get_barrier_semaphore(), 3)


def remote(src, dst, send, recv, device):
    return pltpu.make_async_remote_copy(
        src_ref=src, dst_ref=dst, send_sem=send, recv_sem=recv,
        device_id=device, device_id_type=MESH,
    )


def block_kernel(
    m, taps, group, tokens, gain, w_short, line, skip, w_in, w_out, out,
    xg, sums, wv, wo, acc, hid, gs, toep, stage, got,
    w_sem, ring_send, ring_recv, sib_send, sib_recv, own_send, own_recv,
    keep_sem, give_send, give_recv, rs_send, rs_recv, hid_send, hid_recv,
):
    rows, width = tokens.shape
    half = rows // 2
    piece = half // PIECES
    window = 2 * taps
    per_tile = LANES // group
    tiles = width // LANES
    ring = Ring(m)
    core = ring.core
    ring.greet()

    def w_copy(d):
        base = pl.multiple_of(chip_at((ring.pos + d) % m, m) * 2 * width, 2 * width)
        part = pl.ds(base, 2 * width)
        return pltpu.make_async_copy(w_in.at[:, part, :], wv.at[:, part, :], w_sem.at[d])

    w_copy(0).start()
    wide = tokens[...].astype(jnp.float32)
    xg[ring.pos, core] = (wide * gain[...]).astype(jnp.bfloat16)
    ring.met()

    def view(side, k, q, c):
        if k < PIECES:
            return xg.at[q, c, pl.ds(side * half + k * piece, piece), :]
        return sums.at[q, c, side]

    def hop(s, side, k, q):
        block = view(side, k, q, core)
        return remote(block, block, ring_send.at[s, side, k], ring_recv.at[s, side, k], ring.next[side])

    def across(s, side, k, q, c):
        block = view(side, k, q, c)
        return remote(block, block, sib_send.at[s, side, k], sib_recv.at[s, side, k], ring.sibling)

    parts = [(side, k) for k in range(PIECES) for side in range(2)]
    extra = [(side, PIECES) for side in range(2)]
    every_part = parts + extra
    for side, k in parts:
        hop(0, side, k, ring.pos).start()

    def own(c):
        block = xg.at[ring.pos, c]
        return remote(block, block, own_send.at[0], own_recv.at[0], ring.sibling)

    def own_sums(c):
        block = sums.at[ring.pos, c]
        return remote(block, block, own_send.at[1], own_recv.at[1], ring.sibling)

    own(core).start()
    ones = jnp.ones((8, width), jnp.float32)
    for side in range(2):
        mine = wide[side * half : (side + 1) * half]
        sums[ring.pos, core, side] = lax.dot_general(
            ones, mine * mine, (((1,), (1,)), ((), ())),
            precision=HIGHEST, preferred_element_type=jnp.float32,
        )
        hop(0, side, PIECES, ring.pos).start()
    own_sums(core).start()
    for d in range(1, m // 2 + 1):
        w_copy(d).start()
        if d < m - d:
            w_copy(m - d).start()

    def keep(q):
        base = pl.multiple_of((chip_at(q, m) * 2 + core) * width, width)
        return pltpu.make_async_copy(w_out.at[:, pl.ds(base, width)], wo.at[q, core], keep_sem.at[q])

    def give(q):
        base = pl.multiple_of((chip_at(q, m) * 2 + 1 - core) * width, width)
        return remote(
            w_out.at[:, pl.ds(base, width)], wo.at[q, core], give_send.at[q], give_recv.at[q], ring.sibling
        )

    def multiply(s, first):
        for side in range(2):
            q = ring.behind(side, s)
            here = pl.ds(side * half, half)
            base = pl.multiple_of(chip_at(q, m) * 2 * width, 2 * width)
            for b in range(3):
                term = jnp.dot(
                    xg[q, 0, here, :], wv[b, pl.ds(base, width), :],
                    preferred_element_type=jnp.float32,
                ) + jnp.dot(
                    xg[q, 1, here, :], wv[b, pl.ds(base + width, width), :],
                    preferred_element_type=jnp.float32,
                )
                if first:
                    acc[b, here, :] = term
                else:
                    acc[b, here, :] += term

    def pass_on(s, last):
        for side, k in every_part:
            q = ring.behind(side, s + 1)
            hop(s, side, k, q).wait_recv()
            if not last:
                hop(s + 1, side, k, q).start()
            across(s, side, k, q, core).start()

    def use(s):
        @pl.when(s <= m // 2)
        def _():
            w_copy(s).wait()

        @pl.when(s < m // 2)
        def _():
            w_copy(m - s).wait()

        for side, k in every_part:
            across(s - 1, side, k, ring.behind(side, s), 1 - core).wait_recv()
        multiply(s, False)

    def build(j, carry):
        lines = line[pl.ds(pl.multiple_of(j * per_tile, per_tile), per_tile), :]
        for f in range(per_tile):
            spread = jnp.broadcast_to(lines[f : f + 1, :], (taps, window))
            toep[j, f * taps : (f + 1) * taps, :] = pltpu.roll(
                spread, 0, 1, stride=1, stride_axis=0
            ).astype(jnp.bfloat16)
        return carry

    gs[0:taps, :] = jnp.zeros((taps, LANES), jnp.bfloat16)
    lax.fori_loop(0, tiles, build, 0)
    w_copy(0).wait()
    own(1 - core).wait_recv()
    own_sums(1 - core).wait_recv()
    multiply(0, True)
    pass_on(0, m == 2)

    def gather_step(s, carry):
        keep(s - 1).start()
        give(s - 1).start()
        use(s)
        pass_on(s, False)
        return carry

    lax.fori_loop(1, m - 2, gather_step, 0)
    for q in range(m - 3, m):
        keep(q).start()
        give(q).start()
    use(m - 2)
    pass_on(m - 2, True)
    use(m - 1)

    def total(q, carry):
        return carry + (sums[q, 0] + sums[q, 1])

    squares = lax.fori_loop(0, m, total, jnp.zeros((2, 8, half), jnp.float32))
    factors = lax.rsqrt(squares / w_in.shape[1] + 1e-05)
    factor = jnp.concatenate([factors[0].T[:, 0:1], factors[1].T[:, 0:1]], axis=0)

    def tell(j, c):
        block = hid.at[c, :, pl.ds(pl.multiple_of(j * LANES, LANES), LANES)]
        return remote(block, block, hid_send.at[j], hid_recv.at[j], ring.sibling)

    def tile(j, carry):
        lanes = pl.ds(pl.multiple_of(j * LANES, LANES), LANES)
        at_row = lax.broadcasted_iota(jnp.int32, (rows, LANES), 0)

        def short(b):
            x = acc[b, :, lanes] * factor
            result = w_short[0, pl.ds(b, 1), lanes] * x
            for lag in range(1, w_short.shape[0]):
                moved = jnp.where(at_row >= lag, pltpu.roll(x, lag, 0), 0.0)
                result = result + w_short[lag, pl.ds(b, 1), lanes] * moved
            return result

        gs[taps:, :] = (short(1) * short(2)).astype(jnp.bfloat16)
        query = short(0)
        owner = lax.broadcasted_iota(jnp.int32, (taps, LANES), 1) // group
        for i in range(rows // taps):
            every = jnp.dot(
                toep[j], gs[i * taps : i * taps + window, :], preferred_element_type=jnp.float32
            )
            conv = every[0:taps]
            for f in range(1, per_tile):
                conv = jnp.where(owner == f, every[f * taps : (f + 1) * taps], conv)
            gated = gs[(i + 1) * taps : (i + 2) * taps, :].astype(jnp.float32)
            part = (conv + skip[:, lanes] * gated) * query[i * taps : (i + 1) * taps]
            hid[core, i * taps : (i + 1) * taps, lanes] = part.astype(jnp.bfloat16)
        tell(j, core).start()
        return carry

    lax.fori_loop(0, tiles, tile, 0)

    def arrived(q, carry):
        keep(q).wait()
        block = wo.at[q, 1 - core]
        remote(block, block, give_send.at[q], give_recv.at[q], ring.sibling).wait_recv()
        return carry

    lax.fori_loop(0, m, arrived, 0)
    for j in range(tiles):
        tell(j, 1 - core).wait_recv()

    def span(k):
        return pl.ds(k * piece, piece)

    def reduce_hop(s, side, k):
        return remote(
            stage.at[side, s, span(k), :], got.at[side, s, span(k), :],
            rs_send.at[s, side, k], rs_recv.at[s, side, k], ring.next[side],
        )

    def partial(side, k, q):
        here = pl.ds(side * half + k * piece, piece)
        return jnp.dot(
            hid[0, here, :], wo[q, 0], preferred_element_type=jnp.float32
        ) + jnp.dot(
            hid[1, here, :], wo[q, 1], preferred_element_type=jnp.float32
        )

    for side, k in parts:
        stage[side, 0, span(k), :] = partial(side, k, ring.behind(side, 1)).astype(jnp.bfloat16)
        reduce_hop(0, side, k).start()

    def reduce_step(s, carry):
        for side, k in parts:
            part = partial(side, k, ring.behind(side, s + 1))
            reduce_hop(s - 1, side, k).wait_recv()
            part = part + got[side, s - 1, span(k), :].astype(jnp.float32)
            stage[side, s, span(k), :] = part.astype(jnp.bfloat16)
            reduce_hop(s, side, k).start()
        return carry

    lax.fori_loop(1, m - 1, reduce_step, 0)
    for side, k in parts:
        here = pl.ds(side * half + k * piece, piece)
        part = tokens[here, :].astype(jnp.float32) + partial(side, k, ring.pos)
        reduce_hop(m - 2, side, k).wait_recv()
        part = part + got[side, m - 2, span(k), :].astype(jnp.float32)
        out[here, :] = part.astype(jnp.bfloat16)

    own(core).wait_send()
    own_sums(core).wait_send()

    def settle(s, carry):
        for side, k in every_part:
            hop(s, side, k, ring.behind(side, s)).wait_send()
            across(s, side, k, ring.behind(side, s + 1), core).wait_send()
        for side, k in parts:
            reduce_hop(s, side, k).wait_send()
        return carry

    lax.fori_loop(0, m - 1, settle, 0)

    def given(q, carry):
        give(q).wait_send()
        return carry

    lax.fori_loop(0, m, given, 0)
    for j in range(tiles):
        tell(j, core).wait_send()


def on_device(n, tokens, norm_gain, w_in, w_short, filters, skip, w_out):
    m = n // 2
    rows, width = tokens.shape
    depth = w_in.shape[0]
    count, taps = filters.shape
    group = width // count
    flipped = filters[:, ::-1].astype(jnp.float32)
    line = jnp.pad(flipped, ((0, 0), (1, taps - 1)))
    dma = pltpu.SemaphoreType.DMA
    vmem = pl.BlockSpec(memory_space=pltpu.VMEM)
    hbm = pl.BlockSpec(memory_space=pl.ANY)
    return pl.pallas_call(
        functools.partial(block_kernel, m, taps, group),
        out_shape=jax.ShapeDtypeStruct((rows, width), jnp.bfloat16),
        in_specs=[vmem, vmem, vmem, vmem, vmem, hbm, hbm],
        out_specs=vmem,
        scratch_shapes=[
            pltpu.VMEM((m, 2, rows, width), jnp.bfloat16),
            pltpu.VMEM((m, 2, 2, 8, rows // 2), jnp.float32),
            pltpu.VMEM((3, depth, width), jnp.bfloat16),
            pltpu.VMEM((m, 2, width, width), jnp.bfloat16),
            pltpu.VMEM((3, rows, width), jnp.float32),
            pltpu.VMEM((2, rows, width), jnp.bfloat16),
            pltpu.VMEM((rows + taps, LANES), jnp.bfloat16),
            pltpu.VMEM((width // LANES, LANES // group * taps, 2 * taps), jnp.bfloat16),
            pltpu.VMEM((2, m - 1, rows // 2, width), jnp.bfloat16),
            pltpu.VMEM((2, m - 1, rows // 2, width), jnp.bfloat16),
            dma((m,)),
            dma((m - 1, 2, PIECES + 1)),
            dma((m - 1, 2, PIECES + 1)),
            dma((m - 1, 2, PIECES + 1)),
            dma((m - 1, 2, PIECES + 1)),
            dma((2,)),
            dma((2,)),
            dma((m,)),
            dma((m,)),
            dma((m,)),
            dma((m - 1, 2, PIECES)),
            dma((m - 1, 2, PIECES)),
            dma((width // LANES,)),
            dma((width // LANES,)),
        ],
        compiler_params=pltpu.CompilerParams(
            collective_id=0, has_side_effects=True, vmem_limit_bytes=58 << 20
        ),
        name="hyena_block",
    )(tokens, norm_gain[None, :], w_short, line, skip[None, :], jnp.transpose(w_in, (1, 0, 2)), w_out)


def solution(mesh):
    return jax.shard_map(
        functools.partial(on_device, mesh.shape["tensor"]),
        mesh=mesh,
        in_specs=(
            P("groups", "tensor"),
            P("tensor"),
            P(None, None, "tensor"),
            P(None, None, "tensor"),
            P("tensor", None),
            P("tensor"),
            P("tensor", None),
        ),
        out_specs=P("groups", "tensor"),
        check_vma=False,
    )
```

time: 260 us -> 106 us (0.41)
  Pallas kernels: 186 us -> 102 us
  blocking collectives: 65.3 us -> 0 us
  local copies, waits for them, and re-layouts: 6.83 us -> 2.65 us
    pallas_call x2 -> x1, Pallas kernels: 186 us -> 102 us  [on_device(): pl.pallas_call(functools.partial(block_kernel, m, taps, group), out_shape...]
    psum x1 -> x0, blocking collectives: 65.3 us -> none  [on_device(): squares = lax.psum(jnp.sum(wide * wide, axis=1, keepdims=True), 'tensor')]
    unnamed x13 -> x1, local copies, waits for them, and re-layouts: 5.9 us -> 1.87 us
where the time goes in v2:
time: 106 us; the launch traced here: 105 us
  Pallas kernels  102 us (96%)
  local copies, waits for them, and re-layouts  2.65 us (2%)
    pallas_call x1, Pallas kernels, on_device(): pl.pallas_call(functools.partial(block_kernel, m, taps, group), out_shape...  102 us

profile of v2, /device:TPU:0, one launch (start us, length us, event | category | flops | bytes accessed | tf_op | source)
XLA Modules:
  0.0 105.4 jit_solution(8730756533895981247)
XLA Ops:
  0.0 0.8 rev.3
  0.8 0.7 pad_convert_fusion.line
  1.5 102.1 %hyena_block.1 = bf16[512,512]{1,0:T(8,128)(2,1)} custom-call(bf16[512,512]{1,0:T(8,128)(2,1)} %tokens.1, f32[1,512]{1,0:T(1,128)} %bitcast.4, f32[3,3,512]{2,1,0:T(4,128)} %w_short.1, f32[32,256]{1,0:T(8,128)} %pad_convert_fusion.line, f32[1,512]{1,0:T(1,128)} %bitcast.5, bf16[3,8192,512]{2,1,0:T(8,128)(2,1)} %bitcast.3, bf16[512,8192]{1,0:T(8,128)(2,1)} %w_out.1), custom_call_target="tpu_custom_call" | custom-call | tf_op jit(solution)/shard_map/hyena_block/pallas_call | solution.py:331
  103.6 1.9 %copy.9 = bf16[512,512]{1,0:T(8,128)(2,1)} copy(bf16[512,512]{1,0:T(8,128)(2,1)} %hyena_block.1) | data formatting | bytes 1048576

commit v3 on v2

--- a/solution.py
+++ b/solution.py
@@ -58,8 +58,8 @@
 
 
 def block_kernel(
-    m, taps, group, tokens, gain, w_short, line, skip, w_in, w_out, out,
-    xg, sums, wv, wo, acc, hid, gs, toep, stage, got,
+    m, taps, group, tokens, gain, w_short, filters, skip, w_in, w_out, out,
+    xg, sums, wv, wo, acc, hid, gs, toep, stage, got, line, tail,
     w_sem, ring_send, ring_recv, sib_send, sib_recv, own_send, own_recv,
     keep_sem, give_send, give_recv, rs_send, rs_recv, hid_send, hid_recv,
 ):
@@ -80,7 +80,11 @@
 
     w_copy(0).start()
     wide = tokens[...].astype(jnp.float32)
-    xg[ring.pos, core] = (wide * gain[...]).astype(jnp.bfloat16)
+    scaled = (wide * gain[...]).astype(jnp.bfloat16)
+    for k in range(PIECES):
+        for side in range(2):
+            first = (k * 2 + side) * piece
+            xg[ring.pos, core, pl.ds(side * half + k * piece, piece), :] = scaled[first : first + piece]
     ring.met()
 
     def view(side, k, q, c):
@@ -98,7 +102,7 @@
 
     parts = [(side, k) for k in range(PIECES) for side in range(2)]
     extra = [(side, PIECES) for side in range(2)]
-    every_part = parts + extra
+    every_part = extra + parts
     for side, k in parts:
         hop(0, side, k, ring.pos).start()
 
@@ -113,7 +117,9 @@
     own(core).start()
     ones = jnp.ones((8, width), jnp.float32)
     for side in range(2):
-        mine = wide[side * half : (side + 1) * half]
+        mine = jnp.concatenate(
+            [wide[(k * 2 + side) * piece : (k * 2 + side + 1) * piece] for k in range(PIECES)], axis=0
+        )
         sums[ring.pos, core, side] = lax.dot_general(
             ones, mine * mine, (((1,), (1,)), ((), ())),
             precision=HIGHEST, preferred_element_type=jnp.float32,
@@ -153,8 +159,22 @@
                 else:
                     acc[b, here, :] += term
 
-    def pass_on(s, last):
-        for side, k in every_part:
+    def multiply_piece(s, k):
+        for side in range(2):
+            q = ring.behind(side, s)
+            here = pl.ds(side * half + k * piece, piece)
+            base = pl.multiple_of(chip_at(q, m) * 2 * width, 2 * width)
+            for b in range(3):
+                acc[b, here, :] += jnp.dot(
+                    xg[q, 0, here, :], wv[b, pl.ds(base, width), :],
+                    preferred_element_type=jnp.float32,
+                ) + jnp.dot(
+                    xg[q, 1, here, :], wv[b, pl.ds(base + width, width), :],
+                    preferred_element_type=jnp.float32,
+                )
+
+    def pass_on(s, last, chosen=every_part):
+        for side, k in chosen:
             q = ring.behind(side, s + 1)
             hop(s, side, k, q).wait_recv()
             if not last:
@@ -183,7 +203,13 @@
             ).astype(jnp.bfloat16)
         return carry
 
-    gs[0:taps, :] = jnp.zeros((taps, LANES), jnp.bfloat16)
+    place = lax.broadcasted_iota(jnp.int32, (taps, taps), 0) + lax.broadcasted_iota(jnp.int32, (taps, taps), 1)
+    for side, where in ((0, taps), (1, 0)):
+        line[:, side * taps : (side + 1) * taps] = jnp.dot(
+            filters[...], jnp.where(place == where, 1.0, 0.0).astype(jnp.bfloat16),
+            preferred_element_type=jnp.float32,
+        )
+    gs[0:taps, :] = jnp.zeros((taps, width), jnp.bfloat16)
     lax.fori_loop(0, tiles, build, 0)
     w_copy(0).wait()
     own(1 - core).wait_recv()
@@ -203,49 +229,61 @@
         keep(q).start()
         give(q).start()
     use(m - 2)
-    pass_on(m - 2, True)
-    use(m - 1)
+    def landed(s, chosen):
+        for side, k in chosen:
+            across(s, side, k, ring.behind(side, s + 1), 1 - core).wait_recv()
+
+    def at_piece(k):
+        return [(0, k), (1, k)]
+
+    pass_on(m - 2, True, extra + at_piece(0))
+    landed(m - 2, extra)
 
     def total(q, carry):
         return carry + (sums[q, 0] + sums[q, 1])
 
     squares = lax.fori_loop(0, m, total, jnp.zeros((2, 8, half), jnp.float32))
     factors = lax.rsqrt(squares / w_in.shape[1] + 1e-05)
-    factor = jnp.concatenate([factors[0].T[:, 0:1], factors[1].T[:, 0:1]], axis=0)
-
-    def tell(j, c):
-        block = hid.at[c, :, pl.ds(pl.multiple_of(j * LANES, LANES), LANES)]
-        return remote(block, block, hid_send.at[j], hid_recv.at[j], ring.sibling)
-
-    def tile(j, carry):
+    factor = [factors[side].T[:, 0:1] for side in range(2)]
+    both = 2 * piece
+
+    def tell(k, j, c):
+        block = hid.at[c, pl.ds(k * both, both), pl.ds(pl.multiple_of(j * LANES, LANES), LANES)]
+        return remote(block, block, hid_send.at[k, j], hid_recv.at[k, j], ring.sibling)
+
+    def tile(k, j, carry):
         lanes = pl.ds(pl.multiple_of(j * LANES, LANES), LANES)
-        at_row = lax.broadcasted_iota(jnp.int32, (rows, LANES), 0)
 
         def short(b):
-            x = acc[b, :, lanes] * factor
-            result = w_short[0, pl.ds(b, 1), lanes] * x
+            blocks = [
+                acc[b, side * half + k * piece : side * half + (k + 1) * piece, lanes]
+                * factor[side][k * piece : (k + 1) * piece]
+                for side in range(2)
+            ]
+            before = jnp.zeros((8, LANES), jnp.float32) if k == 0 else tail[b, :, lanes]
+            x = jnp.concatenate([before] + blocks, axis=0)
+            tail[b, :, lanes] = x[both:]
+            result = w_short[0, pl.ds(b, 1), lanes] * x[8:]
             for lag in range(1, w_short.shape[0]):
-                moved = jnp.where(at_row >= lag, pltpu.roll(x, lag, 0), 0.0)
-                result = result + w_short[lag, pl.ds(b, 1), lanes] * moved
+                result = result + w_short[lag, pl.ds(b, 1), lanes] * pltpu.roll(x, lag, 0)[8:]
             return result
 
-        gs[taps:, :] = (short(1) * short(2)).astype(jnp.bfloat16)
+        gs[taps + k * both : taps + (k + 1) * both, lanes] = (short(1) * short(2)).astype(jnp.bfloat16)
         query = short(0)
         owner = lax.broadcasted_iota(jnp.int32, (taps, LANES), 1) // group
-        for i in range(rows // taps):
+        for i in range(both // taps):
+            start = k * both + i * taps
             every = jnp.dot(
-                toep[j], gs[i * taps : i * taps + window, :], preferred_element_type=jnp.float32
+                toep[j], gs[start : start + window, lanes], preferred_element_type=jnp.float32
             )
             conv = every[0:taps]
             for f in range(1, per_tile):
                 conv = jnp.where(owner == f, every[f * taps : (f + 1) * taps], conv)
-            gated = gs[(i + 1) * taps : (i + 2) * taps, :].astype(jnp.float32)
+            gated = gs[start + taps : start + window, lanes].astype(jnp.float32)
             part = (conv + skip[:, lanes] * gated) * query[i * taps : (i + 1) * taps]
-            hid[core, i * taps : (i + 1) * taps, lanes] = part.astype(jnp.bfloat16)
-        tell(j, core).start()
-        return carry
-
-    lax.fori_loop(0, tiles, tile, 0)
+            hid[core, start : start + taps, lanes] = part.astype(jnp.bfloat16)
+        tell(k, j, core).start()
+        return carry
 
     def arrived(q, carry):
         keep(q).wait()
@@ -253,9 +291,6 @@
         remote(block, block, give_send.at[q], give_recv.at[q], ring.sibling).wait_recv()
         return carry
 
-    lax.fori_loop(0, m, arrived, 0)
-    for j in range(tiles):
-        tell(j, 1 - core).wait_recv()
 
     def span(k):
         return pl.ds(k * piece, piece)
@@ -267,16 +302,26 @@
         )
 
     def partial(side, k, q):
-        here = pl.ds(side * half + k * piece, piece)
+        here = pl.ds((k * 2 + side) * piece, piece)
         return jnp.dot(
             hid[0, here, :], wo[q, 0], preferred_element_type=jnp.float32
         ) + jnp.dot(
             hid[1, here, :], wo[q, 1], preferred_element_type=jnp.float32
         )
 
-    for side, k in parts:
-        stage[side, 0, span(k), :] = partial(side, k, ring.behind(side, 1)).astype(jnp.bfloat16)
-        reduce_hop(0, side, k).start()
+    for k in range(PIECES):
+        landed(m - 2, at_piece(k))
+        multiply_piece(m - 1, k)
+        if k + 1 < PIECES:
+            pass_on(m - 2, True, at_piece(k + 1))
+        lax.fori_loop(0, tiles, functools.partial(tile, k), 0)
+        if k == 0:
+            lax.fori_loop(0, m, arrived, 0)
+        for j in range(tiles):
+            tell(k, j, 1 - core).wait_recv()
+        for side in range(2):
+            stage[side, 0, span(k), :] = partial(side, k, ring.behind(side, 1)).astype(jnp.bfloat16)
+            reduce_hop(0, side, k).start()
 
     def reduce_step(s, carry):
         for side, k in parts:
@@ -289,7 +334,7 @@
 
     lax.fori_loop(1, m - 1, reduce_step, 0)
     for side, k in parts:
-        here = pl.ds(side * half + k * piece, piece)
+        here = pl.ds((k * 2 + side) * piece, piece)
         part = tokens[here, :].astype(jnp.float32) + partial(side, k, ring.pos)
         reduce_hop(m - 2, side, k).wait_recv()
         part = part + got[side, m - 2, span(k), :].astype(jnp.float32)
@@ -313,8 +358,9 @@
         return carry
 
     lax.fori_loop(0, m, given, 0)
-    for j in range(tiles):
-        tell(j, core).wait_send()
+    for k in range(PIECES):
+        for j in range(tiles):
+            tell(k, j, core).wait_send()
 
 
 def on_device(n, tokens, norm_gain, w_in, w_short, filters, skip, w_out):
@@ -323,8 +369,6 @@
     depth = w_in.shape[0]
     count, taps = filters.shape
     group = width // count
-    flipped = filters[:, ::-1].astype(jnp.float32)
-    line = jnp.pad(flipped, ((0, 0), (1, taps - 1)))
     dma = pltpu.SemaphoreType.DMA
     vmem = pl.BlockSpec(memory_space=pltpu.VMEM)
     hbm = pl.BlockSpec(memory_space=pl.ANY)
@@ -340,10 +384,12 @@
             pltpu.VMEM((m, 2, width, width), jnp.bfloat16),
             pltpu.VMEM((3, rows, width), jnp.float32),
             pltpu.VMEM((2, rows, width), jnp.bfloat16),
-            pltpu.VMEM((rows + taps, LANES), jnp.bfloat16),
+            pltpu.VMEM((rows + taps, width), jnp.bfloat16),
             pltpu.VMEM((width // LANES, LANES // group * taps, 2 * taps), jnp.bfloat16),
             pltpu.VMEM((2, m - 1, rows // 2, width), jnp.bfloat16),
             pltpu.VMEM((2, m - 1, rows // 2, width), jnp.bfloat16),
+            pltpu.VMEM((count, 2 * taps), jnp.float32),
+            pltpu.VMEM((3, 8, width), jnp.float32),
             dma((m,)),
             dma((m - 1, 2, PIECES + 1)),
             dma((m - 1, 2, PIECES + 1)),
@@ -356,14 +402,14 @@
             dma((m,)),
             dma((m - 1, 2, PIECES)),
             dma((m - 1, 2, PIECES)),
-            dma((width // LANES,)),
-            dma((width // LANES,)),
+            dma((PIECES, width // LANES)),
+            dma((PIECES, width // LANES)),
         ],
         compiler_params=pltpu.CompilerParams(
             collective_id=0, has_side_effects=True, vmem_limit_bytes=58 << 20
         ),
         name="hyena_block",
-    )(tokens, norm_gain[None, :], w_short, line, skip[None, :], jnp.transpose(w_in, (1, 0, 2)), w_out)
+    )(tokens, norm_gain[None, :], w_short, filters, skip[None, :], jnp.transpose(w_in, (1, 0, 2)), w_out)
 
 
 def solution(mesh):

time: 106 us -> 103 us (0.972)
  no operation moved by 1% of the time
where the time goes in v3:
time: 103 us
  Pallas kernels  101 us (98%)
  local copies, waits for them, and re-layouts  1.87 us (2%)
    pallas_call x1, Pallas kernels, on_device(): pl.pallas_call(functools.partial(block_kernel, m, taps, group), out_shape...  101 us

profile of v3, /device:TPU:0, one launch (start us, length us, event | category | flops | bytes accessed | tf_op | source)
XLA Modules:
  0.0 103.1 jit_solution(9477378872152089716)
XLA Ops:
  0.0 101.3 %hyena_block.1 = bf16[512,512]{1,0:T(8,128)(2,1)} custom-call(bf16[512,512]{1,0:T(8,128)(2,1)} %tokens.1, f32[1,512]{1,0:T(1,128)} %bitcast.4, f32[3,3,512]{2,1,0:T(4,128)} %w_short.1, bf16[32,128]{1,0:T(8,128)(2,1)} %filters.1, f32[1,512]{1,0:T(1,128)} %bitcast.5, bf16[3,8192,512]{2,1,0:T(8,128)(2,1)} %bitcast.3, bf16[512,8192]{1,0:T(8,128)(2,1)} %w_out.1), custom_call_target="tpu_custom_call" | custom-call | tf_op jit(solution)/shard_map/hyena_block/pallas_call | solution.py:375
  101.3 1.9 %copy.9 = bf16[512,512]{1,0:T(8,128)(2,1)} copy(bf16[512,512]{1,0:T(8,128)(2,1)} %hyena_block.1) | data formatting | bytes 1048576
